TPU v7x, 32 devices: a whole 2x2x4 slice. The times are simulated.
32 devices in a mesh: rows: 8 (over z, y), modes: 4 (over x, core).
Axes of the slice: x: 2, y: 2, z: 4, core: 2. Of those that a mesh axis runs over, the one named last changes fastest.
Arguments:
- mode_slab: bfloat16 [4096, 512], P('rows', 'modes'), may hold values from -25 to 25
- mass_diag: float32 [4096], P('rows'), may hold values from 9.5 to 19
- mass_gain: float32 [4096], P('rows'), may hold values from 0.5 to 1.5
- band_coef: float32 [4], replicated, may hold values from 0.2 to 0.5
- band_offsets: int32 [4], replicated, may hold values from 1 to 64, as said below
- boundary_blocks: int32 [16, 4], P('rows'), may hold values from 0 to 31, as said below
- boundary_counts: int32 [16], P('rows'), may hold values from 2 to 4, as said below
- boundary_modes: bfloat16 [16, 512, 512], P('rows'), may hold values from -0.5 to 0.5
Outputs:
- projected: bfloat16 [16, 512, 512], P('rows', 'modes')
Inputs may be any that keep to these rules, and one draw needn't show every extreme that they name: `band_offsets`: the offsets are distinct and one of them equals 64. `boundary_blocks`: entries of one component are distinct. For component c with e = c // 2, every entry b (used or not) satisfies (b - e * 4 + 512 // 256) mod (32) < 8. Among the used entries of the components of each index e of rows, one is the block just below e's rows and one the block just above them, counted cyclically. `boundary_counts`: some component uses all 4 blocks.
All inputs are finite; a program needn't handle non-finite values.
Results may differ from a plain program's by a relative error of at most 0.0035.
The roundings to bfloat16 on the way count: a program that leaves them out, or rounds other values in their place, can miss the bound.
Values may be sent and summed in bfloat16 or wider, within the bound.
No kernel may reach another device: no remote copies, remote signals or barrier semaphores. Data moves between devices by JAX's collectives and lax.ppermute only.
A program may use at most 64 MiB of HBM per device.

v0:
```python
import jax
import jax.numpy as jnp
from jax import lax
from jax.sharding import PartitionSpec as P

CB = 512
BLOCK = 128
BMAX = 4
NOFF = 4
BAND = 64


def padded_2(block, sides, width, periodic):
    for axis, dim in sides:
        count = lax.axis_size(axis)
        forward = [(i, i + 1) for i in range(count - 1)]
        if periodic:
            forward.append((count - 1, 0))
        backward = [(target, source) for source, target in forward]
        low = lax.ppermute(
            lax.slice_in_dim(block, block.shape[dim] - width, None, axis=dim), axis, forward
        )
        high = lax.ppermute(lax.slice_in_dim(block, 0, width, axis=dim), axis, backward)
        block = jnp.concatenate([low, block, high], axis=dim)
    return block


def local(
    mode_slab,
    mass_diag,
    mass_gain,
    band_coef,
    band_offsets,
    boundary_blocks,
    boundary_counts,
    boundary_modes,
):
    rows_dev, mode_cols = mode_slab.shape
    per_dev = rows_dev // BLOCK
    rim_rows = per_dev // 2 * BLOCK
    slab_float = mode_slab.astype(jnp.float32)
    scaled = (mass_gain[:, None] * slab_float).astype(jnp.bfloat16)
    padded = padded_2(scaled, (("rows", 0),), BAND, False)
    neighbour = jnp.zeros((rows_dev, mode_cols), jnp.float32)
    for j in range(NOFF):
        offset = band_offsets[j]
        upward = lax.dynamic_slice_in_dim(padded, BAND + offset, rows_dev, 0)
        downward = lax.dynamic_slice_in_dim(padded, BAND - offset, rows_dev, 0)
        neighbour = neighbour + band_coef[j] * (
            upward.astype(jnp.float32) + downward.astype(jnp.float32)
        )
    mass_image = (mass_diag[:, None] * slab_float + mass_gain[:, None] * neighbour).astype(
        jnp.bfloat16
    )
    every_mode = lax.all_gather(mass_image, "modes", axis=1, tiled=True)
    full_order = every_mode.shape[1]
    total_rows = rows_dev * lax.axis_size("rows")
    partial_value = (
        lax.dot_general(
            every_mode, mode_slab, (((0,), (0,)), ((), ())), preferred_element_type=jnp.float32
        )
        / total_rows
    )
    column_block = lax.psum(partial_value, "rows")
    gram_matrix = lax.all_gather(column_block, "modes", axis=1, tiled=True)
    lower_factor = jnp.linalg.cholesky(gram_matrix)
    first_column = lax.axis_index("modes") * mode_cols
    unit_columns = (
        lax.broadcasted_iota(jnp.int32, (full_order, mode_cols), 0)
        == lax.broadcasted_iota(jnp.int32, (full_order, mode_cols), 1) + first_column
    ).astype(jnp.float32)
    inverse = jax.scipy.linalg.solve_triangular(
        lower_factor, unit_columns, lower=True, trans=1
    ).astype(jnp.bfloat16)
    mass_basis = jnp.dot(every_mode, inverse, preferred_element_type=jnp.float32).astype(
        jnp.bfloat16
    )
    extended = padded_2(mass_basis, (("rows", 0),), rim_rows, True)
    total_blocks = per_dev * lax.axis_size("rows")
    window_start = lax.axis_index("rows") * per_dev - per_dev // 2
    local_blocks = jnp.mod(boundary_blocks - window_start, total_blocks)
    owned = boundary_modes.shape[0]
    shaped = boundary_modes.reshape(owned, BMAX, BLOCK, CB)
    row_index = local_blocks[:, :, None] * BLOCK + jnp.arange(BLOCK, dtype=jnp.int32)[None, None, :]
    picked = jnp.take(extended, row_index, axis=0)
    in_use = jnp.arange(BMAX, dtype=jnp.int32)[None, :] < boundary_counts[:, None]
    picked = jnp.where(in_use[:, :, None, None], picked, jnp.zeros_like(picked))
    result = jnp.einsum("csbk,csbm->ckm", picked, shaped, preferred_element_type=jnp.float32)
    return result.astype(jnp.bfloat16)


def solution(mesh):
    in_specs = (
        P("rows", "modes"),
        P("rows"),
        P("rows"),
        P(),
        P(),
        P("rows", None),
        P("rows"),
        P("rows", None, None),
    )
    out_specs = P("rows", "modes", None)
    return jax.shard_map(local, mesh=mesh, in_specs=in_specs, out_specs=out_specs, check_vma=False)
```

profile of v0, /device:TPU:0, one launch (start us, length us, event | category | flops | bytes accessed | tf_op | source)
XLA Modules:
  0.0 294.4 jit_solution(5894387732189599143)
XLA Ops:
  6.5 1.1 fusion.4
  7.7 4.9 %collective-permute-start = (bf16[64,128]{1,0:T(8,128)(2,1)S(1)}, bf16[64,128]{1,0:T(8,128)(2,1)S(1)}, u32[]{:S(2)}, u32[]{:S(2)}) collective-permute-start(bf16[64,128]{1,0:T(8,128)(2,1)S(1)} %get-tuple-element.25), channel_id=1, source_target_pairs={{0,4},{4,8},{8,12},{12,16},{16,20},{20,24},{24,28},{1,5},{5,9},{9,... | collective-permute-start | bytes 49160 | tf_op jit(solution)/shard_map/ppermute | solution.py:20
  12.6 1.3 collective-permute-start.1
  13.9 0.7 fusion.59
  14.6 0.6 fusion.58
  25.6 0.8 copy-done.6
  26.4 2.8 fusion.3
  29.2 7.2 %all_gather.6 = bf16[512,512]{1,0:T(8,128)(2,1)S(1)} all-gather(bf16[512,128]{1,0:T(8,128)(2,1)S(1)} %fusion.3), channel_id=1, replica_groups=mesh['rows'=8,'modes'=4] {'modes'}, dimensions={1}, use_global_device_ids=true | all-gather | bytes 655360 | tf_op jit(solution)/shard_map/all_gather | solution.py:55
  36.4 0.8 copy-done.4
  37.3 1.0 convolution_multiply_fusion
  38.3 72.4 %all-reduce.3.cloned.1.call-done = f32[512,128]{0,1:T(8,128)} async-done(((f32[512,128]{0,1:T(8,128)}), f32[512,128]{0,1:T(8,128)}) %all-reduce.3.cloned.1.call-update) | async-done | bytes 262160 | tf_op jit(solution)/shard_map/psum | solution.py:64
  110.7 0.6 iota_multiply_fusion
  111.3 0.7 copy-done.12
  112.1 0.7 fusion.44
  112.8 15.5 %all-gather.2.cloned.1.call-done = f32[512,512]{0,1:T(8,128)} async-done(((f32[512,128]{0,1:T(8,128)}), f32[512,512]{0,1:T(8,128)}) %all-gather.2.cloned.1.call-update) | async-done | bytes 1048592 | tf_op jit(solution)/shard_map/all_gather | solution.py:65
  128.4 1.6 copy.13
  130.0 0.2 fusion.1
  130.3 1.0 copy-done.2
  131.3 11.7 %cholesky.104 = f32[128,128]{1,0:T(8,128)S(1)} custom-call(f32[128,128]{1,0:T(8,128)S(1)} %cholesky.266), custom_call_target="Cholesky" | custom-call | tf_op jit(solution)/shard_map/jit(cholesky)/cholesky | solution.py:66
  143.1 9.8 %custom-call.31 = f32[1,128,128]{1,2,0:T(8,128)S(1)} custom-call(f32[1,128,128]{2,1,0:T(8,128)S(1)} %get-tuple-element.36), custom_call_target="InvertDiagBlocksLowerTriangular" | custom-call | tf_op jit(solution)/shard_map/jit(cholesky)/cholesky | solution.py:66
  153.0 0.3 constant_dynamic-update-slice_fusion
  153.3 0.3 convolution_subtract_fusion
  153.6 0.7 copy-done.7
  154.3 11.7 %cholesky.217 = f32[128,128]{1,0:T(8,128)S(1)} custom-call(f32[128,128]{1,0:T(8,128)S(1)} %cholesky.270), custom_call_target="Cholesky" | custom-call | tf_op jit(solution)/shard_map/jit(cholesky)/cholesky | solution.py:66
  166.1 9.9 %custom-call.32 = f32[1,128,128]{1,2,0:T(8,128)S(1)} custom-call(f32[1,128,128]{2,1,0:T(8,128)S(1)} %get-tuple-element.33), custom_call_target="InvertDiagBlocksLowerTriangular" | custom-call | tf_op jit(solution)/shard_map/jit(cholesky)/cholesky | solution.py:66
  176.0 1.2 convolution_dynamic-update-slice_fusion
  177.2 0.4 convolution_subtract_fusion.1
  177.6 0.6 cholesky.275
  178.2 13.2 %cholesky.238 = f32[128,128]{1,0:T(8,128)} custom-call(f32[128,128]{1,0:T(8,128)} %cholesky.275), custom_call_target="Cholesky" | custom-call | tf_op jit(solution)/shard_map/jit(cholesky)/cholesky | solution.py:66
  191.4 1.5 select_reduce_fusion.1
  192.9 0.7 compare_reduce_fusion.1
  193.6 11.3 %custom-call.33 = f32[1,128,128]{1,2,0:T(8,128)} custom-call(f32[1,128,128]{2,1,0:T(8,128)} %get-tuple-element.30), custom_call_target="InvertDiagBlocksLowerTriangular" | custom-call | tf_op jit(solution)/shard_map/jit(cholesky)/cholesky | solution.py:66
  204.8 1.0 convolution_dynamic-update-slice_fusion.1
  205.9 0.4 convolution_subtract_fusion.5
  206.3 11.7 %cholesky.255 = f32[128,128]{1,0:T(8,128)S(1)} custom-call(f32[128,128]{1,0:T(8,128)S(1)} %convolution_subtract_fusion.5), custom_call_target="Cholesky" | custom-call | tf_op jit(solution)/shard_map/jit(cholesky)/cholesky | solution.py:66
  218.0 0.3 select_reduce_fusion
  218.2 0.7 compare_reduce_fusion
  218.9 0.7 compare_reduce_fusion.2
  222.1 0.1 select_select_fusion
  222.3 0.5 copy-done.14
  222.8 9.9 %while.1 = (s32[]{:T(128)}, f32[512,512]{1,0:T(8,128)S(1)}, s32[4,2]{0,1:T(2,128)S(1)}, f32[4,128,128]{2,1,0:T(8,128)}, s32[]{:T(128)}) while((s32[]{:T(128)}, f32[512,512]{1,0:T(8,128)S(1)}, s32[4,2]{0,1:T(2,128)S(1)}, f32[4,128,128]{2,1,0:T(8,128)}, s32[]{:T(128)}) %tuple.39), condition=%wide.while_cond, body=%wide.while_body.sunk | while | flops 2 | bytes 132705 | solution.py:72
  222.8 0.5 fusion.73
  223.4 1.9 bitcast_dynamic-update-slice_fusion.2
  225.3 0.5 fusion.73
  225.8 1.9 bitcast_dynamic-update-slice_fusion.2
  227.8 0.5 fusion.73
  228.3 1.9 bitcast_dynamic-update-slice_fusion.2
  230.2 0.5 fusion.73
  230.8 1.9 bitcast_dynamic-update-slice_fusion.2
  232.6 40.1 %custom-call.34 = f32[4,128,128]{1,2,0:T(8,128)S(1)} custom-call(f32[4,128,128]{2,1,0:T(8,128)} %get-tuple-element.12), custom_call_target="InvertDiagBlocksLowerTriangular" | custom-call | tf_op jit(solution)/shard_map/jit(_solve_triangular)/triangular_solve | solution.py:72
  272.8 0.9 fusion.60
  273.6 0.3 convolution_subtract_fusion.3
  273.9 0.2 fusion.61
  274.2 0.4 convolution_subtract_fusion.2
  274.6 0.2 fusion.62
  274.8 0.5 convolution_subtract_fusion.4
  275.3 0.2 convolution_convert_fusion.1
  275.6 0.3 convolution_convert_fusion
  275.9 1.5 collective-permute-start.2
  277.4 3.3 %collective-permute-start.3 = (bf16[256,128]{1,0:T(8,128)(2,1)S(1)}, bf16[256,128]{1,0:T(8,128)(2,1)S(1)}, u32[]{:S(2)}, u32[]{:S(2)}) collective-permute-start(bf16[256,128]{1,0:T(8,128)(2,1)S(1)} %get-tuple-element.24), channel_id=1, source_target_pairs={{4,0},{8,4},{12,8},{16,12},{20,16},{24,20},{28,24},{0,28},{5,1},{9... | collective-permute-start | bytes 196616 | tf_op jit(solution)/shard_map/ppermute | solution.py:23
  280.8 2.2 collective-permute-done.2
  283.1 3.2 %gather_fusion = bf16[1024,128]{1,0:T(8,128)(2,1)S(1)} fusion(bf16[1024,128]{1,0:T(8,128)(2,1)S(1)} %pad_maximum_fusion, s32[1024]{0:T(1024)S(1)} %broadcast_clamp_fusion), kind=kCustom, calls=%fused_computation | custom fusion | bytes 528384 | tf_op jit(solution)/shard_map/jit(_take)/gather | solution.py:85
  286.3 0.2 copy.14
  286.5 1.1 fusion
  (52 shorter events, 1.1 us)
Async XLA Ops:
  6.5 280.0 %copy-start = (bf16[2,512,512]{2,1,0:T(8,128)(2,1)S(1)}, bf16[2,512,512]{2,1,0:T(8,128)(2,1)}, u32[]{:S(2)}) copy-start(bf16[2,512,512]{2,1,0:T(8,128)(2,1)} %param.15) | copy-start | bytes 3145732
  6.5 104.1 %all-reduce.3.cloned.1.call-start = ((), (), s32[]{:S(2)}) async-start(), calls=%async_computation | async-start | bytes 524288 | tf_op jit(solution)/shard_map/psum | solution.py:64
  7.7 6.2 %copy-start.9 = (s32[4]{0:T(128)S(1)}, s32[4]{0:T(128)}, u32[]{:S(2)}) copy-start(s32[4]{0:T(128)} %param.12) | copy-start | bytes 52
  7.7 17.8 %collective-permute-start = (bf16[64,128]{1,0:T(8,128)(2,1)S(1)}, bf16[64,128]{1,0:T(8,128)(2,1)S(1)}, u32[]{:S(2)}, u32[]{:S(2)}) collective-permute-start(bf16[64,128]{1,0:T(8,128)(2,1)S(1)} %get-tuple-element.25), channel_id=1, source_target_pairs={{0,4},{4,8},{8,12},{12,16},{16,20},{20,24},{24,28},{1,5},{5,9},{9,... | collective-permute-start | bytes 49160 | tf_op jit(solution)/shard_map/ppermute | solution.py:20
  12.6 12.9 %collective-permute-start.1 = (bf16[64,128]{1,0:T(8,128)(2,1)S(1)}, bf16[64,128]{1,0:T(8,128)(2,1)S(1)}, u32[]{:S(2)}, u32[]{:S(2)}) collective-permute-start(bf16[64,128]{1,0:T(8,128)(2,1)S(1)} %get-tuple-element.26), channel_id=1, source_target_pairs={{4,0},{8,4},{12,8},{16,12},{20,16},{24,20},{28,24},{5,1},{9,5},{13... | collective-permute-start | bytes 49160 | tf_op jit(solution)/shard_map/ppermute | solution.py:23
  13.9 0.7 copy-start.10
  25.5 0.9 copy-start.6
  25.6 0.9 copy-start.11
  25.6 0.8 copy-start.8
  36.4 0.8 copy-start.4
  38.3 90.1 %all-gather.2.cloned.1.call-start = ((), (), s32[]{:S(2)}) async-start(), calls=%async_computation.1 | async-start | bytes 1310720 | tf_op jit(solution)/shard_map/all_gather | solution.py:65
  111.3 0.7 copy-start.12
  128.4 1.7 copy-start.1
  130.2 1.0 copy-start.2
  131.2 21.7 %copy-start.3 = (f32[512,512]{1,0:T(8,128)S(1)}, f32[512,512]{1,0:T(8,128)}, u32[]{:S(2)}) copy-start(f32[512,512]{1,0:T(8,128)} %copy-done.2) | copy-start | bytes 3145732
  153.6 0.7 copy-start.7
  222.1 0.7 copy-start.14
  274.5 1.0 copy-start.5
  275.9 4.8 %copy-start.13 = (s32[2]{0:T(128)S(1)}, s32[2]{0:T(128)}, u32[]{:S(2)}) copy-start(s32[2]{0:T(128)} %param.14) | copy-start | bytes 28
  275.9 7.1 %collective-permute-start.2 = (bf16[256,128]{1,0:T(8,128)(2,1)S(1)}, bf16[256,128]{1,0:T(8,128)(2,1)S(1)}, u32[]{:S(2)}, u32[]{:S(2)}) collective-permute-start(bf16[256,128]{1,0:T(8,128)(2,1)S(1)} %get-tuple-element.23), channel_id=1, source_target_pairs={{0,4},{4,8},{8,12},{12,16},{16,20},{20,24},{24,28},{28,0},{1,5},{5... | collective-permute-start | bytes 196616 | tf_op jit(solution)/shard_map/ppermute | solution.py:20
  277.4 5.7 %collective-permute-start.3 = (bf16[256,128]{1,0:T(8,128)(2,1)S(1)}, bf16[256,128]{1,0:T(8,128)(2,1)S(1)}, u32[]{:S(2)}, u32[]{:S(2)}) collective-permute-start(bf16[256,128]{1,0:T(8,128)(2,1)S(1)} %get-tuple-element.24), channel_id=1, source_target_pairs={{4,0},{8,4},{12,8},{16,12},{20,16},{24,20},{28,24},{0,28},{5,1},{9... | collective-permute-start | bytes 196616 | tf_op jit(solution)/shard_map/ppermute | solution.py:23
Sparse Core Ops, SparseCore 0:
  38.4 72.2 all-reduce.2
  112.3 15.9 all-gather.1
where the time goes:
time: 295 us; the launch traced here: 294 us
  other arithmetic  129 us (44%)
  waiting for transfers between devices  90.3 us (31%)
  between operations  26.6 us (9%)
  local copies, waits for them, and re-layouts  21.7 us (7%)
  starting transfers between devices  11 us (4%)
  matrix products  8.59 us (3%)
  blocking collectives  7.2 us (2%)
    another operation x14, other arithmetic, local(): lower_factor = jnp.linalg.cholesky(gram_matrix)  83.2 us
    psum x1, waiting for transfers between devices, local(): column_block = lax.psum(partial_value, 'rows')  72.4 us
    another operation x3, other arithmetic, local(): jax.scipy.linalg.solve_triangular(lower_factor, unit_columns, lower=True,...  40.8 us
    all_gather x1, waiting for transfers between devices, local(): gram_matrix = lax.all_gather(column_block, 'modes', axis=1, tiled=True)  15.5 us
    another operation x12, local copies, waits for them, and re-layouts  9.85 us
    all_gather x1, blocking collectives, local(): every_mode = lax.all_gather(mass_image, 'modes', axis=1, tiled=True)  7.2 us
    ppermute x2, starting transfers between devices, padded_2(): lax.ppermute(lax.slice_in_dim(block, block.shape[dim] - width, None, axis...  6.39 us
  transfers between devices with their start and end apart: 6, of which 4 were waited for; matrix products, arithmetic and copies ran while one was open for 1% of the time, Pallas kernels for 0%

commit v1 on v0

--- a/solution.py
+++ b/solution.py
@@ -1,3 +1,4 @@
+import functools
 import jax
 import jax.numpy as jnp
 from jax import lax
@@ -8,6 +9,22 @@
 BMAX = 4
 NOFF = 4
 BAND = 64
+
+
+def play_lanes_for(field_in, mesh_dim):
+    degree = lax.axis_size(mesh_dim)
+    pieces_in = [field_in]
+    for at in range(degree - 1):
+        y1 = lax.ppermute(
+            pieces_in[-1], axis_name=mesh_dim, perm=[(w, (w + 1) % degree) for w in range(degree)]
+        )
+        pieces_in.append(y1)
+    reached = jnp.concatenate(pieces_in[::-1], axis=1)
+    piece_out = lax.axis_index(mesh_dim)
+    return jnp.roll(reached, (piece_out + 1) * field_in.shape[1], axis=1)
+
+
+wait_edges_over_axis = functools.partial(play_lanes_for, mesh_dim="modes")
 
 
 def padded_2(block, sides, width, periodic):
@@ -62,7 +79,7 @@
         / total_rows
     )
     column_block = lax.psum(partial_value, "rows")
-    gram_matrix = lax.all_gather(column_block, "modes", axis=1, tiled=True)
+    gram_matrix = wait_edges_over_axis(column_block)
     lower_factor = jnp.linalg.cholesky(gram_matrix)
     first_column = lax.axis_index("modes") * mode_cols
     unit_columns = (

time: 295 us -> 294 us (level)
  other arithmetic: 129 us -> 126 us
    ppermute x0 -> x3, waiting for transfers between devices: none -> 17.4 us  [play_lanes_for(): lax.ppermute(pieces_in[-1], axis_name=mesh_dim, perm=[(w, (w + 1) % degre...]
    all_gather x1 -> x0, waiting for transfers between devices: 15.5 us -> none  [local(): gram_matrix = lax.all_gather(column_block, 'modes', axis=1, tiled=True)]
    another operation x14, other arithmetic: 83.2 us -> 78.7 us  [local(): lower_factor = jnp.linalg.cholesky(gram_matrix)]
  transfers between devices with their start and end apart: 6 -> 8, of which waited for: 4 -> 5; matrix products, arithmetic and copies ran while one was open for 1% -> 1% of each run, Pallas kernels for 0% -> 0%
where the time goes in v1:
time: 294 us; the launch traced here: 293 us
  other arithmetic  126 us (43%)
  waiting for transfers between devices  92 us (31%)
  between operations  26.4 us (9%)
  local copies, waits for them, and re-layouts  20.9 us (7%)
  starting transfers between devices  10.9 us (4%)
  matrix products  9.77 us (3%)
  blocking collectives  7.2 us (2%)
    another operation x14, other arithmetic, local(): lower_factor = jnp.linalg.cholesky(gram_matrix)  78.7 us
    psum x1, waiting for transfers between devices, local(): column_block = lax.psum(partial_value, 'rows')  72.4 us
    another operation x3, other arithmetic, local(): jax.scipy.linalg.solve_triangular(lower_factor, unit_columns, lower=True,...  40.2 us
    ppermute x3, waiting for transfers between devices, play_lanes_for(): lax.ppermute(pieces_in[-1], axis_name=mesh_dim, perm=[(w, (w + 1) % degre...  17.4 us
    another operation x12, local copies, waits for them, and re-layouts  10.8 us
    all_gather x1, blocking collectives, local(): every_mode = lax.all_gather(mass_image, 'modes', axis=1, tiled=True)  7.2 us
  transfers between devices with their start and end apart: 8, of which 5 were waited for; matrix products, arithmetic and copies ran while one was open for 1% of the time, Pallas kernels for 0%

profile of v1, /device:TPU:0, one launch (start us, length us, event | category | flops | bytes accessed | tf_op | source)
XLA Modules:
  0.0 292.8 jit_solution(7338169038316625728)
XLA Ops:
  6.5 1.1 fusion.4
  7.7 4.9 %collective-permute-start = (bf16[64,128]{1,0:T(8,128)(2,1)S(1)}, bf16[64,128]{1,0:T(8,128)(2,1)S(1)}, u32[]{:S(2)}, u32[]{:S(2)}) collective-permute-start(bf16[64,128]{1,0:T(8,128)(2,1)S(1)} %get-tuple-element.25), channel_id=1, source_target_pairs={{0,4},{4,8},{8,12},{12,16},{16,20},{20,24},{24,28},{1,5},{5,9},{9,... | collective-permute-start | bytes 49160 | tf_op jit(solution)/shard_map/ppermute | solution.py:37
  12.6 1.3 collective-permute-start.1
  13.9 1.4 fusion.59
  15.3 1.5 fusion.58
  27.0 3.9 %fusion.3 = bf16[512,128]{1,0:T(8,128)(2,1)S(1)} fusion(bf16[512,128]{1,0:T(8,128)(2,1)} %param.8, bf16[640,128]{1,0:T(8,128)(2,1)S(1)} %pad_maximum_fusion.1, s32[]{:T(128)S(6)} %select_n.80, s32[]{:T(128)S(6)} %select_n.79, f32[]{:T(128)} %bitcast.15, s32[]{:T(128)S(6)} %select_n.78, s32[]{:T(128)S(6)} %select_n.77, f32[]{:T(128)} %bitcast.10, ...), kind=kLoop, calls=%fused_computation.23 | loop fusion | flops 1572864 | bytes 1314864 | tf_op jit(solution)/shard_map/convert_element_type | solution.py:69
  30.8 7.2 %all_gather.3 = bf16[512,512]{1,0:T(8,128)(2,1)S(1)} all-gather(bf16[512,128]{1,0:T(8,128)(2,1)S(1)} %fusion.3), channel_id=1, replica_groups=mesh['rows'=8,'modes'=4] {'modes'}, dimensions={1}, use_global_device_ids=true | all-gather | bytes 655360 | tf_op jit(solution)/shard_map/all_gather | solution.py:72
  38.0 0.8 copy-done.3
  38.8 1.0 convolution_multiply_fusion
  39.9 72.4 %all-reduce.3.cloned.1.call-done = f32[512,128]{0,1:T(8,128)} async-done(((f32[512,128]{0,1:T(8,128)}), f32[512,128]{0,1:T(8,128)}) %all-reduce.3.cloned.1.call-update) | async-done | bytes 262160 | tf_op jit(solution)/shard_map/psum | solution.py:81
  112.3 0.1 fusion.47
  112.4 0.1 compare_select_fusion
  112.4 5.9 %collective-permute-done.2 = f32[512,128]{0,1:T(8,128)S(1)} collective-permute-done((f32[512,128]{0,1:T(8,128)}, f32[512,128]{0,1:T(8,128)S(1)}, u32[]{:S(2)}, u32[]{:S(2)}) %collective-permute-start.2) | collective-permute-done | bytes 262176 | tf_op jit(solution)/shard_map/ppermute | solution.py:18
  118.3 5.8 %collective-permute-done.3 = f32[512,128]{0,1:T(8,128)S(1)} collective-permute-done((f32[512,128]{0,1:T(8,128)S(1)}, f32[512,128]{0,1:T(8,128)S(1)}, u32[]{:S(2)}, u32[]{:S(2)}) %collective-permute-start.3) | collective-permute-done | bytes 262176 | tf_op jit(solution)/shard_map/ppermute | solution.py:18
  124.2 5.7 %collective-permute-done.4 = f32[512,128]{0,1:T(8,128)S(1)} collective-permute-done((f32[512,128]{0,1:T(8,128)S(1)}, f32[512,128]{0,1:T(8,128)S(1)}, u32[]{:S(2)}, u32[]{:S(2)}) %collective-permute-start.4) | collective-permute-done | bytes 262176 | tf_op jit(solution)/shard_map/ppermute | solution.py:18
  130.1 1.3 copy-done.2
  131.5 0.3 copy.13
  131.9 1.4 fusion.1
  133.3 1.0 copy-done.1
  134.2 11.7 %cholesky.104 = f32[128,128]{1,0:T(8,128)S(1)} custom-call(f32[128,128]{1,0:T(8,128)S(1)} %cholesky.266), custom_call_target="Cholesky" | custom-call | tf_op jit(solution)/shard_map/jit(cholesky)/cholesky | solution.py:83
  146.0 0.1 cholesky.224
  146.1 9.8 %custom-call.31 = f32[1,128,128]{1,2,0:T(8,128)S(1)} custom-call(f32[1,128,128]{2,1,0:T(8,128)S(1)} %get-tuple-element.36), custom_call_target="InvertDiagBlocksLowerTriangular" | custom-call | tf_op jit(solution)/shard_map/jit(cholesky)/cholesky | solution.py:83
  155.9 1.2 constant_dynamic-update-slice_fusion.8
  157.2 1.3 convolution_subtract_fusion
  158.5 11.7 %cholesky.217 = f32[128,128]{1,0:T(8,128)S(1)} custom-call(f32[128,128]{1,0:T(8,128)S(1)} %cholesky.270), custom_call_target="Cholesky" | custom-call | tf_op jit(solution)/shard_map/jit(cholesky)/cholesky | solution.py:83
  170.2 9.9 %custom-call.32 = f32[1,128,128]{1,2,0:T(8,128)S(1)} custom-call(f32[1,128,128]{2,1,0:T(8,128)S(1)} %get-tuple-element.33), custom_call_target="InvertDiagBlocksLowerTriangular" | custom-call | tf_op jit(solution)/shard_map/jit(cholesky)/cholesky | solution.py:83
  180.2 0.3 convolution_dynamic-update-slice_fusion
  180.4 1.3 convolution_subtract_fusion.1
  181.7 11.7 %cholesky.238 = f32[128,128]{1,0:T(8,128)S(1)} custom-call(f32[128,128]{1,0:T(8,128)S(1)} %cholesky.275), custom_call_target="Cholesky" | custom-call | tf_op jit(solution)/shard_map/jit(cholesky)/cholesky | solution.py:83
  193.5 0.7 compare_reduce_fusion.1
  194.1 9.8 %custom-call.33 = f32[1,128,128]{1,2,0:T(8,128)S(1)} custom-call(f32[1,128,128]{2,1,0:T(8,128)S(1)} %get-tuple-element.30), custom_call_target="InvertDiagBlocksLowerTriangular" | custom-call | tf_op jit(solution)/shard_map/jit(cholesky)/cholesky | solution.py:83
  204.0 0.2 convolution_dynamic-update-slice_fusion.1
  204.2 1.2 convolution_subtract_fusion.5
  205.4 11.9 %cholesky.255 = f32[128,128]{1,0:T(8,128)S(1)} custom-call(f32[128,128]{1,0:T(8,128)S(1)} %convolution_subtract_fusion.5), custom_call_target="Cholesky" | custom-call | tf_op jit(solution)/shard_map/jit(cholesky)/cholesky | solution.py:83
  217.3 0.7 compare_reduce_fusion
  218.0 0.7 compare_reduce_fusion.2
  221.1 0.1 select_select_fusion
  221.2 10.8 %while.1 = (s32[]{:T(128)}, f32[512,512]{1,0:T(8,128)S(1)}, s32[4,2]{0,1:T(2,128)S(1)}, f32[4,128,128]{2,1,0:T(8,128)}, s32[]{:T(128)}) while((s32[]{:T(128)}, f32[512,512]{1,0:T(8,128)S(1)}, s32[4,2]{0,1:T(2,128)S(1)}, f32[4,128,128]{2,1,0:T(8,128)}, s32[]{:T(128)}) %tuple.39), condition=%wide.while_cond, body=%wide.while_body.sunk | while | flops 2 | bytes 132705 | solution.py:89
  221.2 0.1 constant_dynamic-slice_fusion.3
  221.3 0.6 fusion.73
  221.9 2.0 bitcast_dynamic-update-slice_fusion.2
  223.9 0.1 constant_dynamic-slice_fusion.3
  224.0 0.6 fusion.73
  224.6 2.0 bitcast_dynamic-update-slice_fusion.2
  226.7 0.6 fusion.73
  227.3 2.0 bitcast_dynamic-update-slice_fusion.2
  229.4 0.6 fusion.73
  230.0 2.0 bitcast_dynamic-update-slice_fusion.2
  232.0 40.1 %custom-call.34 = f32[4,128,128]{1,2,0:T(8,128)S(1)} custom-call(f32[4,128,128]{2,1,0:T(8,128)} %get-tuple-element.12), custom_call_target="InvertDiagBlocksLowerTriangular" | custom-call | tf_op jit(solution)/shard_map/jit(_solve_triangular)/triangular_solve | solution.py:89
  272.1 0.2 fusion.60
  272.3 0.3 convolution_subtract_fusion.3
  272.6 0.2 fusion.61
  272.8 0.4 convolution_subtract_fusion.2
  273.2 0.2 fusion.62
  273.4 0.5 convolution_subtract_fusion.4
  273.9 0.2 convolution_convert_fusion.1
  274.2 0.3 convolution_convert_fusion
  274.5 0.8 collective-permute-start.5
  275.3 4.0 %collective-permute-start.6 = (bf16[256,128]{1,0:T(8,128)(2,1)S(1)}, bf16[256,128]{1,0:T(8,128)(2,1)S(1)}, u32[]{:S(2)}, u32[]{:S(2)}) collective-permute-start(bf16[256,128]{1,0:T(8,128)(2,1)S(1)} %get-tuple-element.24), channel_id=1, source_target_pairs={{4,0},{8,4},{12,8},{16,12},{20,16},{24,20},{28,24},{0,28},{5,1},{9... | collective-permute-start | bytes 196616 | tf_op jit(solution)/shard_map/ppermute | solution.py:40
  279.3 0.1 iota_compare_fusion.4
  279.3 2.2 collective-permute-done.5
  281.5 3.2 %gather_fusion = bf16[1024,128]{1,0:T(8,128)(2,1)S(1)} fusion(bf16[1024,128]{1,0:T(8,128)(2,1)S(1)} %pad_maximum_fusion, s32[1024]{0:T(1024)S(1)} %broadcast_clamp_fusion), kind=kCustom, calls=%fused_computation | custom fusion | bytes 528384 | tf_op jit(solution)/shard_map/jit(_take)/gather | solution.py:102
  284.7 0.2 copy.14
  284.9 1.1 fusion
  (52 shorter events, 0.7 us)
Async XLA Ops:
  6.5 278.4 %copy-start = (bf16[2,512,512]{2,1,0:T(8,128)(2,1)S(1)}, bf16[2,512,512]{2,1,0:T(8,128)(2,1)}, u32[]{:S(2)}) copy-start(bf16[2,512,512]{2,1,0:T(8,128)(2,1)} %param.15) | copy-start | bytes 3145732
  6.5 32.3 %copy-start.5 = (bf16[512,128]{1,0:T(8,128)(2,1)S(1)}, bf16[512,128]{1,0:T(8,128)(2,1)}, u32[]{:S(2)}) copy-start(bf16[512,128]{1,0:T(8,128)(2,1)} %param.8) | copy-start | bytes 393220
  6.5 33.3 %copy-start.7 = (s32[2,4]{1,0:T(2,128)S(1)}, s32[2,4]{1,0:T(2,128)}, u32[]{:S(2)}) copy-start(s32[2,4]{1,0:T(2,128)} %param.13) | copy-start | bytes 100
  6.5 105.7 %all-reduce.3.cloned.1.call-start = ((), (), s32[]{:S(2)}) async-start(), calls=%async_computation | async-start | bytes 524288 | tf_op jit(solution)/shard_map/psum | solution.py:81
  7.7 19.2 %collective-permute-start = (bf16[64,128]{1,0:T(8,128)(2,1)S(1)}, bf16[64,128]{1,0:T(8,128)(2,1)S(1)}, u32[]{:S(2)}, u32[]{:S(2)}) collective-permute-start(bf16[64,128]{1,0:T(8,128)(2,1)S(1)} %get-tuple-element.25), channel_id=1, source_target_pairs={{0,4},{4,8},{8,12},{12,16},{16,20},{20,24},{24,28},{1,5},{5,9},{9,... | collective-permute-start | bytes 49160 | tf_op jit(solution)/shard_map/ppermute | solution.py:37
  12.6 14.4 %collective-permute-start.1 = (bf16[64,128]{1,0:T(8,128)(2,1)S(1)}, bf16[64,128]{1,0:T(8,128)(2,1)S(1)}, u32[]{:S(2)}, u32[]{:S(2)}) collective-permute-start(bf16[64,128]{1,0:T(8,128)(2,1)S(1)} %get-tuple-element.26), channel_id=1, source_target_pairs={{4,0},{8,4},{12,8},{16,12},{20,16},{24,20},{28,24},{5,1},{9,5},{13... | collective-permute-start | bytes 49160 | tf_op jit(solution)/shard_map/ppermute | solution.py:40
  38.0 0.8 copy-start.3
  112.3 17.7 %copy-start.6 = (f32[512,128]{0,1:T(8,128)S(1)}, f32[512,128]{0,1:T(8,128)}, u32[]{:S(2)}) copy-start(f32[512,128]{0,1:T(8,128)} %all-reduce.3.cloned.1.call-done) | copy-start | bytes 786436
  112.3 6.0 %collective-permute-start.2 = (f32[512,128]{0,1:T(8,128)}, f32[512,128]{0,1:T(8,128)S(1)}, u32[]{:S(2)}, u32[]{:S(2)}) collective-permute-start(f32[512,128]{0,1:T(8,128)} %all-reduce.3.cloned.1.call-done), channel_id=1, source_target_pairs={{0,1},{1,2},{2,3},{3,0},{4,5},{5,6},{6,7},{7,4},{8,9},{9,10},{10,1... | collective-permute-start | bytes 786440 | tf_op jit(solution)/shard_map/ppermute | solution.py:18
  118.3 5.8 %collective-permute-start.3 = (f32[512,128]{0,1:T(8,128)S(1)}, f32[512,128]{0,1:T(8,128)S(1)}, u32[]{:S(2)}, u32[]{:S(2)}) collective-permute-start(f32[512,128]{0,1:T(8,128)S(1)} %collective-permute-done.2), channel_id=1, source_target_pairs={{0,1},{1,2},{2,3},{3,0},{4,5},{5,6},{6,7},{7,4},{8,9},{9,10},{10,1... | collective-permute-start | bytes 786440 | tf_op jit(solution)/shard_map/ppermute | solution.py:18
  124.1 5.8 %collective-permute-start.4 = (f32[512,128]{0,1:T(8,128)S(1)}, f32[512,128]{0,1:T(8,128)S(1)}, u32[]{:S(2)}, u32[]{:S(2)}) collective-permute-start(f32[512,128]{0,1:T(8,128)S(1)} %collective-permute-done.3), channel_id=1, source_target_pairs={{0,1},{1,2},{2,3},{3,0},{4,5},{5,6},{6,7},{7,4},{8,9},{9,10},{10,1... | collective-permute-start | bytes 786440 | tf_op jit(solution)/shard_map/ppermute | solution.py:18
  130.1 1.3 copy-start.2
  133.3 1.0 copy-start.1
  221.2 53.0 %copy-start.4 = (bf16[512,512]{1,0:T(8,128)(2,1)S(1)}, bf16[512,512]{1,0:T(8,128)(2,1)}, u32[]{:S(2)}) copy-start(bf16[512,512]{1,0:T(8,128)(2,1)} %copy-done.3) | copy-start | bytes 1572868
  221.2 58.1 %copy-start.8 = (s32[2]{0:T(128)S(1)}, s32[2]{0:T(128)}, u32[]{:S(2)}) copy-start(s32[2]{0:T(128)} %param.14) | copy-start | bytes 28
  274.5 7.0 %collective-permute-start.5 = (bf16[256,128]{1,0:T(8,128)(2,1)S(1)}, bf16[256,128]{1,0:T(8,128)(2,1)S(1)}, u32[]{:S(2)}, u32[]{:S(2)}) collective-permute-start(bf16[256,128]{1,0:T(8,128)(2,1)S(1)} %get-tuple-element.23), channel_id=1, source_target_pairs={{0,4},{4,8},{8,12},{12,16},{16,20},{20,24},{24,28},{28,0},{1,5},{5... | collective-permute-start | bytes 196616 | tf_op jit(solution)/shard_map/ppermute | solution.py:37
  275.3 6.2 %collective-permute-start.6 = (bf16[256,128]{1,0:T(8,128)(2,1)S(1)}, bf16[256,128]{1,0:T(8,128)(2,1)S(1)}, u32[]{:S(2)}, u32[]{:S(2)}) collective-permute-start(bf16[256,128]{1,0:T(8,128)(2,1)S(1)} %get-tuple-element.24), channel_id=1, source_target_pairs={{4,0},{8,4},{12,8},{16,12},{20,16},{24,20},{28,24},{0,28},{5,1},{9... | collective-permute-start | bytes 196616 | tf_op jit(solution)/shard_map/ppermute | solution.py:40
Sparse Core Ops, SparseCore 0:
  40.0 72.2 all-reduce.2
